TPU v7x, 32 devices: a whole 2x2x4 slice. The times are simulated.
32 devices in a mesh: grp: 4 (over y, x), leaf: 8 (over z, core).
Axes of the slice: x: 2, y: 2, z: 4, core: 2. Of those that a mesh axis runs over, the one named last changes fastest.
Arguments:
- direction: bfloat16 [49152, 256], P(('grp', 'leaf')), may hold values from -6 to 6
- residual: bfloat16 [49152, 256], P(('grp', 'leaf')), may hold values from -6 to 6
- leaf_order: int32 [32, 1536], P(('grp', 'leaf')), may hold values from 0 to 1535, as said below
- diag_block: bfloat16 [32, 1536, 1536], P(('grp', 'leaf')), may hold values from -0.15625 to 0.15625
- up_basis: bfloat16 [32, 1536, 128], P(('grp', 'leaf')), may hold values from -0.15625 to 0.15625
- down_basis: bfloat16 [32, 1536, 128], P(('grp', 'leaf')), may hold values from -0.5 to 0.5
- leaf_ops: bfloat16 [3, 32, 128, 128], P(None, ('grp', 'leaf')), may hold values from -0.375 to 0.375
- inner_ops: bfloat16 [3, 24, 128, 128], P(None, 'grp'), may hold values from -0.375 to 0.375
- top_ops: bfloat16 [3, 6, 128, 128], replicated, may hold values from -0.375 to 0.375
- ridge_shift: float32 [1], replicated, may hold values from 0.5 to 2
Outputs:
- image: bfloat16 [49152, 256], P(('grp', 'leaf'))
- curvature_gram: float32 [256, 256], replicated
- residual_gram: float32 [256, 256], replicated
Inputs may be any that keep to these rules, and one draw needn't show every extreme that they name: Each row of leaf_order is a permutation of 0 to 1535.
All inputs are finite; a program needn't handle non-finite values.
Results may differ from a plain program's by a relative error of at most 0.022.
Values may be sent and summed in bfloat16 or wider, within the bound.
No kernel may reach another device: no remote copies, remote signals or barrier semaphores. Data moves between devices by JAX's collectives and lax.ppermute only.
A program may use at most 64 MiB of HBM per device.

v0:
```python
import jax
import jax.numpy as jnp
from jax import lax
from jax.sharding import PartitionSpec as P


def from_partner(block, axis, apart):
    count = lax.axis_size(axis)
    route = []
    for low in range(count):
        high = low | 1 << apart
        if high != low and high < count:
            route += [(low, high), (high, low)]
    return lax.ppermute(block, axis, route)


def lift_single(transfer, skeleton):
    return jnp.einsum("rs,rk->sk", transfer, skeleton, preferred_element_type=jnp.float32).astype(
        jnp.bfloat16
    )


def body(
    direction,
    residual,
    leaf_order,
    diag_block,
    up_basis,
    down_basis,
    leaf_ops,
    inner_ops,
    top_ops,
    ridge_shift,
):
    leaves_here = lax.axis_size("leaf")
    groups = lax.axis_size("grp")
    leaf_levels = leaves_here.bit_length() - 1
    group_levels = groups.bit_length() - 1
    total_levels = leaf_levels + group_levels
    my_leaf = lax.axis_index("leaf")
    my_group = lax.axis_index("grp")
    ordering = leaf_order[0]
    ordered = jnp.take(direction, ordering, axis=0)
    skeleton = jnp.einsum(
        "nr,nk->rk", up_basis[0], ordered, preferred_element_type=jnp.float32
    ).astype(jnp.bfloat16)

    def inner_offset(height):
        return sum((leaves_here >> section for section in range(1, height)))

    def top_offset(upper_level):
        return sum((groups >> section for section in range(upper_level)))

    def path_operators(height):
        if height == 0:
            return leaf_ops[:, 0]
        if height < leaf_levels:
            return lax.dynamic_index_in_dim(
                inner_ops, inner_offset(height) + (my_leaf >> height), 1, keepdims=False
            )
        upper_level = height - leaf_levels
        return lax.dynamic_index_in_dim(
            top_ops, top_offset(upper_level) + (my_group >> upper_level), 1, keepdims=False
        )

    contrib = lift_single(leaf_ops[0, 0], skeleton)
    siblings = []
    for bit_index in range(leaf_levels):
        other_skeleton, other_contrib = from_partner((skeleton, contrib), "leaf", bit_index)
        siblings.append(other_skeleton)
        skeleton = (contrib.astype(jnp.float32) + other_contrib.astype(jnp.float32)).astype(
            jnp.bfloat16
        )
        contrib = lift_single(path_operators(bit_index + 1)[0], skeleton)
    for bit_index in range(group_levels):
        other_skeleton, other_contrib = from_partner((skeleton, contrib), "grp", bit_index)
        siblings.append(other_skeleton)
        if bit_index + 1 < group_levels:
            skeleton = (contrib.astype(jnp.float32) + other_contrib.astype(jnp.float32)).astype(
                jnp.bfloat16
            )
            contrib = lift_single(path_operators(leaf_levels + bit_index + 1)[0], skeleton)
    coarse = jnp.zeros((up_basis.shape[2], direction.shape[1]), jnp.bfloat16)
    for height in reversed(range(total_levels)):
        operators = path_operators(height)
        coupled = jnp.dot(operators[2], siblings[height], preferred_element_type=jnp.float32)
        passed = jnp.dot(operators[1], coarse, preferred_element_type=jnp.float32)
        coarse = (coupled + passed).astype(jnp.bfloat16)
    local = jnp.dot(diag_block[0], ordered, preferred_element_type=jnp.float32)
    local = local + jnp.dot(down_basis[0], coarse, preferred_element_type=jnp.float32)
    restored = jnp.zeros(local.shape, jnp.float32).at[ordering].set(local)
    image = (restored + ridge_shift[0] * direction.astype(jnp.float32)).astype(jnp.bfloat16)
    curvature_part = jnp.einsum("nk,nm->km", direction, image, preferred_element_type=jnp.float32)
    correlation_part = jnp.einsum("nk,nm->km", residual, image, preferred_element_type=jnp.float32)
    curvature, correlation = lax.psum((curvature_part, correlation_part), ("grp", "leaf"))
    points_total = direction.shape[0] * leaves_here * groups
    return (image, curvature / points_total, correlation / points_total)


def solution(mesh):
    return jax.shard_map(
        body,
        mesh=mesh,
        in_specs=(
            P(("grp", "leaf"), None),
            P(("grp", "leaf"), None),
            P(("grp", "leaf"), None),
            P(("grp", "leaf"), None, None),
            P(("grp", "leaf"), None, None),
            P(("grp", "leaf"), None, None),
            P(None, ("grp", "leaf"), None, None),
            P(None, "grp", None, None),
            P(),
            P(),
        ),
        out_specs=(P(("grp", "leaf"), None), P(), P()),
        check_vma=False,
    )
```

profile of v0, /device:TPU:0, one launch (start us, length us, event | category | flops | bytes accessed | tf_op | source)
XLA Modules:
  0.0 201.7 jit_solution(530703202432133354)
XLA Ops:
  8.8 4.9 %gather_fusion = bf16[1536,256]{1,0:T(8,128)(2,1)S(1)} fusion(bf16[1536,256]{1,0:T(8,128)(2,1)} %param.10, s32[2048]{0:T(1024)S(1)} %pad_clamp_fusion), kind=kCustom, calls=%fused_computation | custom fusion | bytes 1579008 | tf_op jit(solution)/shard_map/jit(_take)/gather | solution.py:43
  16.2 1.0 convolution_convert_fusion.3
  17.2 3.0 %collective-permute-start.3 = (bf16[128,256]{1,0:T(8,128)(2,1)S(1)}, bf16[128,256]{1,0:T(8,128)(2,1)S(1)}, u32[]{:S(2)}, u32[]{:S(2)}) collective-permute-start(bf16[128,256]{1,0:T(8,128)(2,1)S(1)} %convolution_convert_fusion.3), channel_id=1, source_target_pairs={{0,2},{2,0},{1,3},{3,1},{4,6},{6,4},{5,7},{7,5},{8,10},{10,8},{9,1... | collective-permute-start | bytes 196616 | tf_op jit(solution)/shard_map/ppermute | solution.py:14
  20.2 2.4 %collective-permute-done.3 = bf16[128,256]{1,0:T(8,128)(2,1)S(1)} collective-permute-done((bf16[128,256]{1,0:T(8,128)(2,1)S(1)}, bf16[128,256]{1,0:T(8,128)(2,1)S(1)}, u32[]{:S(2)}, u32[]{:S(2)}) %collective-permute-start.3) | collective-permute-done | bytes 65568 | tf_op jit(solution)/shard_map/ppermute | solution.py:14
  23.6 2.9 %collective-permute-start.5 = (bf16[128,256]{1,0:T(8,128)(2,1)S(1)}, bf16[128,256]{1,0:T(8,128)(2,1)S(1)}, u32[]{:S(2)}, u32[]{:S(2)}) collective-permute-start(bf16[128,256]{1,0:T(8,128)(2,1)S(1)} %convolution_convert_fusion.2), channel_id=1, source_target_pairs={{0,4},{4,0},{1,5},{5,1},{2,6},{6,2},{3,7},{7,3},{8,12},{12,8},{9,1... | collective-permute-start | bytes 196616 | tf_op jit(solution)/shard_map/ppermute | solution.py:14
  26.5 2.3 %collective-permute-done.5 = bf16[128,256]{1,0:T(8,128)(2,1)S(1)} collective-permute-done((bf16[128,256]{1,0:T(8,128)(2,1)S(1)}, bf16[128,256]{1,0:T(8,128)(2,1)S(1)}, u32[]{:S(2)}, u32[]{:S(2)}) %collective-permute-start.5) | collective-permute-done | bytes 65568 | tf_op jit(solution)/shard_map/ppermute | solution.py:14
  28.9 1.0 convolution_convert_fusion.1
  29.8 1.8 collective-permute-start.7
  31.6 5.3 %fusion = f32[256,1536]{1,0:T(8,128)} fusion(bf16[1,1536,1536]{2,1,0:T(8,128)(2,1)} %param.13, bf16[1536,256]{1,0:T(8,128)(2,1)S(1)} %gather_fusion, pred[1536]{0:T(1024)(128)(4,1)S(1)} %compare_and_fusion), kind=kOutput, calls=%fused_computation.2 | convolution fusion | flops 1208352768 | bytes 7079424 | tf_op jit(solution)/shard_map/dot_general | solution.py:89
  37.6 1.6 collective-permute-start.8
  40.1 1.6 collective-permute-start.2
  41.7 3.2 %collective-permute-start.4 = (bf16[128,256]{1,0:T(8,128)(2,1)S(1)}, bf16[128,256]{1,0:T(8,128)(2,1)S(1)}, u32[]{:S(2)}, u32[]{:S(2)}) collective-permute-start(bf16[128,256]{1,0:T(8,128)(2,1)S(1)} %add_convert_fusion.3), channel_id=1, source_target_pairs={{0,4},{4,0},{1,5},{5,1},{2,6},{6,2},{3,7},{7,3},{8,12},{12,8},{9,1... | collective-permute-start | bytes 196616 | tf_op jit(solution)/shard_map/ppermute | solution.py:14
  45.4 1.1 fusion.9
  46.5 2.6 %collective-permute-done.6 = bf16[128,256]{1,0:T(8,128)(2,1)S(1)} collective-permute-done((bf16[128,256]{1,0:T(8,128)(2,1)S(1)}, bf16[128,256]{1,0:T(8,128)(2,1)S(1)}, u32[]{:S(2)}, u32[]{:S(2)}) %collective-permute-start.6) | collective-permute-done | bytes 65568 | tf_op jit(solution)/shard_map/ppermute | solution.py:14
  49.1 1.1 fusion.10
  50.2 1.1 fusion.11
  51.3 1.1 fusion.12
  52.5 1.9 fusion.2
  54.4 1.6 copy.16
  56.0 7.8 %scatter_custom_fusion = f32[1536,256]{1,0:T(8,128)S(1)} fusion(s32[1536]{0:T(1024)S(1)} %fusion.27, f32[1536,256]{1,0:T(8,128)} %copy.16, f32[]{:T(128)} %constant.47.clone.1), kind=kCustom, calls=%fused_computation.29 | custom fusion | bytes 1573376 | tf_op jit(solution)/shard_map/scatter | solution.py:91
  64.1 1.1 convolution_bitcast_fusion.1
  65.2 1.1 convolution_bitcast_fusion
  66.3 125.8 %all-reduce.3.cloned.1.call-done = (f32[256,256]{0,1:T(8,128)}, f32[256,256]{0,1:T(8,128)}) async-done(((f32[256,256]{0,1:T(8,128)}, f32[256,256]{0,1:T(8,128)}), (f32[256,256]{0,1:T(8,128)}, f32[256,256]{0,1:T(8,128)})) %all-reduce.3.cloned.1.call-update) | async-done | bytes 524304 | tf_op jit(solution)/shard_map/psum | solution.py:95
  192.1 1.1 broadcast_multiply_fusion
  (38 shorter events, 8.4 us)
Async XLA Ops:
  7.2 58.0 %copy-start = (bf16[1536,256]{1,0:T(8,128)(2,1)S(1)}, bf16[1536,256]{1,0:T(8,128)(2,1)}, u32[]{:S(2)}) copy-start(bf16[1536,256]{1,0:T(8,128)(2,1)} %param.11) | copy-start | bytes 2359300
  7.2 184.9 %all-reduce.3.cloned.1.call-start = ((), (), s32[]{:S(2)}) async-start(), calls=%async_computation | async-start | bytes 1048576 | tf_op jit(solution)/shard_map/psum | solution.py:95
  8.8 5.0 %copy-start.5 = (bf16[1,1536,128]{2,1,0:T(8,128)(2,1)S(1)}, bf16[1,1536,128]{2,1,0:T(8,128)(2,1)}, u32[]{:S(2)}) copy-start(bf16[1,1536,128]{2,1,0:T(8,128)(2,1)} %param.14) | copy-start | bytes 1179652
  13.7 0.9 copy-start.4
  14.8 1.5 collective-permute-start.1
  17.2 5.4 %collective-permute-start.3 = (bf16[128,256]{1,0:T(8,128)(2,1)S(1)}, bf16[128,256]{1,0:T(8,128)(2,1)S(1)}, u32[]{:S(2)}, u32[]{:S(2)}) collective-permute-start(bf16[128,256]{1,0:T(8,128)(2,1)S(1)} %convolution_convert_fusion.3), channel_id=1, source_target_pairs={{0,2},{2,0},{1,3},{3,1},{4,6},{6,4},{5,7},{7,5},{8,10},{10,8},{9,1... | collective-permute-start | bytes 196616 | tf_op jit(solution)/shard_map/ppermute | solution.py:14
  23.6 5.3 %collective-permute-start.5 = (bf16[128,256]{1,0:T(8,128)(2,1)S(1)}, bf16[128,256]{1,0:T(8,128)(2,1)S(1)}, u32[]{:S(2)}, u32[]{:S(2)}) collective-permute-start(bf16[128,256]{1,0:T(8,128)(2,1)S(1)} %convolution_convert_fusion.2), channel_id=1, source_target_pairs={{0,4},{4,0},{1,5},{5,1},{2,6},{6,2},{3,7},{7,3},{8,12},{12,8},{9,1... | collective-permute-start | bytes 196616 | tf_op jit(solution)/shard_map/ppermute | solution.py:14
  26.5 25.9 %collective-permute-start = (bf16[128,256]{0,1:T(8,128)(2,1)S(1)}, bf16[128,256]{0,1:T(8,128)(2,1)S(1)}, u32[]{:S(2)}, u32[]{:S(2)}) collective-permute-start(bf16[128,256]{0,1:T(8,128)(2,1)S(1)} %bitcast.82), channel_id=1, source_target_pairs={{0,1},{1,0},{2,3},{3,2},{4,5},{5,4},{6,7},{7,6},{8,9},{9,8},{10,11... | collective-permute-start | bytes 196616 | tf_op jit(solution)/shard_map/ppermute | solution.py:14
  29.8 7.8 %collective-permute-start.7 = (bf16[128,256]{1,0:T(8,128)(2,1)S(1)}, bf16[128,256]{1,0:T(8,128)(2,1)S(1)}, u32[]{:S(2)}, u32[]{:S(2)}) collective-permute-start(bf16[128,256]{1,0:T(8,128)(2,1)S(1)} %convolution_convert_fusion.1), channel_id=1, source_target_pairs={{0,8},{8,0},{16,24},{24,16},{1,9},{9,1},{17,25},{25,17},{2,10},{10... | collective-permute-start | bytes 196616 | tf_op jit(solution)/shard_map/ppermute | solution.py:14
  36.9 15.6 %copy-start.3 = (bf16[1,1536,128]{2,1,0:T(8,128)(2,1)S(1)}, bf16[1,1536,128]{2,1,0:T(8,128)(2,1)}, u32[]{:S(2)}) copy-start(bf16[1,1536,128]{2,1,0:T(8,128)(2,1)} %param.15) | copy-start | bytes 1179652
  37.6 7.8 %collective-permute-start.8 = (bf16[128,256]{1,0:T(8,128)(2,1)S(1)}, bf16[128,256]{1,0:T(8,128)(2,1)S(1)}, u32[]{:S(2)}, u32[]{:S(2)}) collective-permute-start(bf16[128,256]{1,0:T(8,128)(2,1)S(1)} %add_convert_fusion.1), channel_id=1, source_target_pairs={{0,16},{16,0},{8,24},{24,8},{1,17},{17,1},{9,25},{25,9},{2,18},{18... | collective-permute-start | bytes 196616 | tf_op jit(solution)/shard_map/ppermute | solution.py:14
  40.1 11.2 %collective-permute-start.2 = (bf16[128,256]{0,1:T(8,128)(2,1)S(1)}, bf16[128,256]{0,1:T(8,128)(2,1)S(1)}, u32[]{:S(2)}, u32[]{:S(2)}) collective-permute-start(bf16[128,256]{0,1:T(8,128)(2,1)S(1)} %add_convert_fusion.4), channel_id=1, source_target_pairs={{0,2},{2,0},{1,3},{3,1},{4,6},{6,4},{5,7},{7,5},{8,10},{10,8},{9,1... | collective-permute-start | bytes 196616 | tf_op jit(solution)/shard_map/ppermute | solution.py:14
  41.7 8.5 %collective-permute-start.4 = (bf16[128,256]{1,0:T(8,128)(2,1)S(1)}, bf16[128,256]{1,0:T(8,128)(2,1)S(1)}, u32[]{:S(2)}, u32[]{:S(2)}) collective-permute-start(bf16[128,256]{1,0:T(8,128)(2,1)S(1)} %add_convert_fusion.3), channel_id=1, source_target_pairs={{0,4},{4,0},{1,5},{5,1},{2,6},{6,2},{3,7},{7,3},{8,12},{12,8},{9,1... | collective-permute-start | bytes 196616 | tf_op jit(solution)/shard_map/ppermute | solution.py:14
  44.8 4.3 %collective-permute-start.6 = (bf16[128,256]{1,0:T(8,128)(2,1)S(1)}, bf16[128,256]{1,0:T(8,128)(2,1)S(1)}, u32[]{:S(2)}, u32[]{:S(2)}) collective-permute-start(bf16[128,256]{1,0:T(8,128)(2,1)S(1)} %add_convert_fusion.2), channel_id=1, source_target_pairs={{0,8},{8,0},{16,24},{24,16},{1,9},{9,1},{17,25},{25,17},{2,10},{10... | collective-permute-start | bytes 196616 | tf_op jit(solution)/shard_map/ppermute | solution.py:14
  56.0 7.8 %copy-start.1 = (bf16[1536,256]{1,0:T(8,128)(2,1)S(1)}, bf16[1536,256]{1,0:T(8,128)(2,1)}, u32[]{:S(2)}) copy-start(bf16[1536,256]{1,0:T(8,128)(2,1)} %param.10) | copy-start | bytes 2359300
  64.0 1.1 copy-start.2
Sparse Core Ops, SparseCore 0:
  66.4 125.6 all-reduce.2
where the time goes:
time: 203 us; the launch traced here: 202 us
  waiting for transfers between devices  134 us (66%)
  matrix products  18.4 us (9%)
  local copies, waits for them, and re-layouts  16.2 us (8%)
  starting transfers between devices  15.2 us (7%)
  between operations  14.9 us (7%)
  other arithmetic  2.88 us (1%)
    psum x1, waiting for transfers between devices, body(): lax.psum((curvature_part, correlation_part), ('grp', 'leaf'))  126 us
    ppermute x9, starting transfers between devices, from_partner(): return lax.ppermute(block, axis, route)  15.1 us
    ppermute x9, waiting for transfers between devices, from_partner(): return lax.ppermute(block, axis, route)  8.29 us
    scatter x1, local copies, waits for them, and re-layouts, body(): restored = jnp.zeros(local.shape, jnp.float32).at[ordering].set(local)  7.8 us
    dot_general x5, matrix products, body(): passed = jnp.dot(operators[1], coarse, preferred_element_type=jnp.float32)  5.26 us
    dot_general x1, matrix products, body(): local = jnp.dot(diag_block[0], ordered, preferred_element_type=jnp.float32)  5.26 us
    gather x1, local copies, waits for them, and re-layouts, body(): ordered = jnp.take(direction, ordering, axis=0)  4.93 us
  transfers between devices with their start and end apart: 10, of which 5 were waited for; matrix products, arithmetic and copies ran while one was open for 6% of the time, Pallas kernels for 0%

commit v1 on v0

--- a/solution.py
+++ b/solution.py
@@ -92,7 +92,7 @@
     image = (restored + ridge_shift[0] * direction.astype(jnp.float32)).astype(jnp.bfloat16)
     curvature_part = jnp.einsum("nk,nm->km", direction, image, preferred_element_type=jnp.float32)
     correlation_part = jnp.einsum("nk,nm->km", residual, image, preferred_element_type=jnp.float32)
-    curvature, correlation = lax.psum((curvature_part, correlation_part), ("grp", "leaf"))
+    curvature, correlation = lax.psum(lax.psum((curvature_part, correlation_part), "leaf"), "grp")
     points_total = direction.shape[0] * leaves_here * groups
     return (image, curvature / points_total, correlation / points_total)
 

time: 203 us -> 177 us (0.87)
  waiting for transfers between devices: 134 us -> 109 us
    psum x1 -> x2, waiting for transfers between devices: 126 us -> 101 us  [the longest x1 53 us: body(): lax.psum((curvature_part, correlation_part), 'leaf')]
  transfers between devices with their start and end apart: 10 -> 11, of which waited for: 5 -> 6; matrix products, arithmetic and copies ran while one was open for 6% -> 7% of each run, Pallas kernels for 0% -> 0%
where the time goes in v1:
time: 177 us
  waiting for transfers between devices  109 us (62%)
  matrix products  18.4 us (10%)
  local copies, waits for them, and re-layouts  16.3 us (9%)
  starting transfers between devices  15.2 us (9%)
  between operations  14.9 us (8%)
  other arithmetic  2.88 us (2%)
    psum x1, waiting for transfers between devices, body(): lax.psum((curvature_part, correlation_part), 'leaf')  53 us
    psum x1, waiting for transfers between devices, body(): lax.psum(lax.psum((curvature_part, correlation_part), 'leaf'), 'grp')  47.5 us
    ppermute x9, starting transfers between devices, from_partner(): return lax.ppermute(block, axis, route)  15.1 us
    ppermute x9, waiting for transfers between devices, from_partner(): return lax.ppermute(block, axis, route)  8.29 us
    scatter x1, local copies, waits for them, and re-layouts, body(): restored = jnp.zeros(local.shape, jnp.float32).at[ordering].set(local)  7.8 us
    dot_general x1, matrix products, body(): local = jnp.dot(diag_block[0], ordered, preferred_element_type=jnp.float32)  5.27 us
    dot_general x5, matrix products, body(): passed = jnp.dot(operators[1], coarse, preferred_element_type=jnp.float32)  5.26 us
    gather x1, local copies, waits for them, and re-layouts, body(): ordered = jnp.take(direction, ordering, axis=0)  4.93 us
  transfers between devices with their start and end apart: 11, of which 6 were waited for; matrix products, arithmetic and copies ran while one was open for 7% of the time, Pallas kernels for 0%

profile of v1, /device:TPU:0, one launch (start us, length us, event | category | flops | bytes accessed | tf_op | source)
XLA Modules:
  0.0 176.5 jit_solution(14040519780217156872)
XLA Ops:
  8.8 4.9 %gather_fusion = bf16[1536,256]{1,0:T(8,128)(2,1)S(1)} fusion(bf16[1536,256]{1,0:T(8,128)(2,1)} %param.10, s32[2048]{0:T(1024)S(1)} %pad_clamp_fusion), kind=kCustom, calls=%fused_computation | custom fusion | bytes 1579008 | tf_op jit(solution)/shard_map/jit(_take)/gather | solution.py:43
  16.2 1.0 convolution_convert_fusion.3
  17.2 3.0 %collective-permute-start.3 = (bf16[128,256]{1,0:T(8,128)(2,1)S(1)}, bf16[128,256]{1,0:T(8,128)(2,1)S(1)}, u32[]{:S(2)}, u32[]{:S(2)}) collective-permute-start(bf16[128,256]{1,0:T(8,128)(2,1)S(1)} %convolution_convert_fusion.3), channel_id=1, source_target_pairs={{0,2},{2,0},{1,3},{3,1},{4,6},{6,4},{5,7},{7,5},{8,10},{10,8},{9,1... | collective-permute-start | bytes 196616 | tf_op jit(solution)/shard_map/ppermute | solution.py:14
  20.2 2.4 %collective-permute-done.3 = bf16[128,256]{1,0:T(8,128)(2,1)S(1)} collective-permute-done((bf16[128,256]{1,0:T(8,128)(2,1)S(1)}, bf16[128,256]{1,0:T(8,128)(2,1)S(1)}, u32[]{:S(2)}, u32[]{:S(2)}) %collective-permute-start.3) | collective-permute-done | bytes 65568 | tf_op jit(solution)/shard_map/ppermute | solution.py:14
  23.6 2.9 %collective-permute-start.5 = (bf16[128,256]{1,0:T(8,128)(2,1)S(1)}, bf16[128,256]{1,0:T(8,128)(2,1)S(1)}, u32[]{:S(2)}, u32[]{:S(2)}) collective-permute-start(bf16[128,256]{1,0:T(8,128)(2,1)S(1)} %convolution_convert_fusion.2), channel_id=1, source_target_pairs={{0,4},{4,0},{1,5},{5,1},{2,6},{6,2},{3,7},{7,3},{8,12},{12,8},{9,1... | collective-permute-start | bytes 196616 | tf_op jit(solution)/shard_map/ppermute | solution.py:14
  26.5 2.3 %collective-permute-done.5 = bf16[128,256]{1,0:T(8,128)(2,1)S(1)} collective-permute-done((bf16[128,256]{1,0:T(8,128)(2,1)S(1)}, bf16[128,256]{1,0:T(8,128)(2,1)S(1)}, u32[]{:S(2)}, u32[]{:S(2)}) %collective-permute-start.5) | collective-permute-done | bytes 65568 | tf_op jit(solution)/shard_map/ppermute | solution.py:14
  29.8 1.8 %collective-permute-start.7 = (bf16[128,256]{1,0:T(8,128)(2,1)S(1)}, bf16[128,256]{1,0:T(8,128)(2,1)S(1)}, u32[]{:S(2)}, u32[]{:S(2)}) collective-permute-start(bf16[128,256]{1,0:T(8,128)(2,1)S(1)} %convolution_convert_fusion.1), channel_id=1, source_target_pairs={{0,8},{8,0},{16,24},{24,16},{1,9},{9,1},{17,25},{25,17},{2,10},{10... | collective-permute-start | bytes 196616 | tf_op jit(solution)/shard_map/ppermute | solution.py:14
  31.6 5.3 %fusion = f32[256,1536]{1,0:T(8,128)} fusion(bf16[1,1536,1536]{2,1,0:T(8,128)(2,1)} %param.13, bf16[1536,256]{1,0:T(8,128)(2,1)S(1)} %gather_fusion, pred[1536]{0:T(1024)(128)(4,1)S(1)} %compare_and_fusion), kind=kOutput, calls=%fused_computation.2 | convolution fusion | flops 1208352768 | bytes 7079424 | tf_op jit(solution)/shard_map/dot_general | solution.py:89
  37.6 1.6 collective-permute-start.8
  40.1 1.6 collective-permute-start.2
  41.7 3.2 %collective-permute-start.4 = (bf16[128,256]{1,0:T(8,128)(2,1)S(1)}, bf16[128,256]{1,0:T(8,128)(2,1)S(1)}, u32[]{:S(2)}, u32[]{:S(2)}) collective-permute-start(bf16[128,256]{1,0:T(8,128)(2,1)S(1)} %add_convert_fusion.3), channel_id=1, source_target_pairs={{0,4},{4,0},{1,5},{5,1},{2,6},{6,2},{3,7},{7,3},{8,12},{12,8},{9,1... | collective-permute-start | bytes 196616 | tf_op jit(solution)/shard_map/ppermute | solution.py:14
  45.4 1.1 fusion.9
  46.5 2.6 %collective-permute-done.6 = bf16[128,256]{1,0:T(8,128)(2,1)S(1)} collective-permute-done((bf16[128,256]{1,0:T(8,128)(2,1)S(1)}, bf16[128,256]{1,0:T(8,128)(2,1)S(1)}, u32[]{:S(2)}, u32[]{:S(2)}) %collective-permute-start.6) | collective-permute-done | bytes 65568 | tf_op jit(solution)/shard_map/ppermute | solution.py:14
  49.1 1.1 fusion.10
  50.2 1.1 fusion.11
  51.3 1.1 fusion.12
  52.5 1.9 %fusion.2 = f32[1536,256]{0,1:T(8,128)S(1)} fusion(f32[256,1536]{1,0:T(8,128)} %fusion, f32[256,128]{1,0:T(8,128)S(1)} %fusion.12, bf16[128,256]{0,1:T(8,128)(2,1)S(1)} %collective-permute-done, bf16[1,1536,128]{2,1,0:T(8,128)(2,1)S(1)} %copy-done.3, bf16[3,1,128,128]{3,2,1,0:T(8,128)(2,1)S(1)} %copy-done.4), kind=kOutput, calls=%fused_computation.5 | convolution fusion | flops 109510656 | bytes 3768320 | tf_op jit(solution)/shard_map/dot_general | solution.py:90
  54.4 1.6 copy.16
  56.0 7.8 %scatter_custom_fusion = f32[1536,256]{1,0:T(8,128)S(1)} fusion(s32[1536]{0:T(1024)S(1)} %fusion.27, f32[1536,256]{1,0:T(8,128)} %copy.16, f32[]{:T(128)} %constant.47.clone.1), kind=kCustom, calls=%fused_computation.29 | custom fusion | bytes 1573376 | tf_op jit(solution)/shard_map/scatter | solution.py:91
  64.1 1.1 convolution_bitcast_fusion.1
  65.2 1.1 convolution_bitcast_fusion
  66.4 53.0 %all-reduce.5.cloned.1.call-done = (f32[256,256]{0,1:T(8,128)}, f32[256,256]{0,1:T(8,128)}) async-done(((f32[256,256]{0,1:T(8,128)}, f32[256,256]{0,1:T(8,128)}), (f32[256,256]{0,1:T(8,128)}, f32[256,256]{0,1:T(8,128)})) %all-reduce.5.cloned.1.call-update) | async-done | bytes 524304 | tf_op jit(solution)/shard_map/psum | solution.py:95
  119.5 47.5 %all-reduce.7.cloned.1.call-done = (f32[256,256]{0,1:T(8,128)}, f32[256,256]{0,1:T(8,128)}) async-done(((f32[256,256]{0,1:T(8,128)}, f32[256,256]{0,1:T(8,128)}), (f32[256,256]{0,1:T(8,128)}, f32[256,256]{0,1:T(8,128)})) %all-reduce.7.cloned.1.call-update) | async-done | bytes 524304 | tf_op jit(solution)/shard_map/psum | solution.py:95
  166.9 1.1 broadcast_multiply_fusion
  (41 shorter events, 9.4 us)
Async XLA Ops:
  7.2 58.0 %copy-start = (bf16[1536,256]{1,0:T(8,128)(2,1)S(1)}, bf16[1536,256]{1,0:T(8,128)(2,1)}, u32[]{:S(2)}) copy-start(bf16[1536,256]{1,0:T(8,128)(2,1)} %param.11) | copy-start | bytes 2359300
  7.2 112.3 %all-reduce.5.cloned.1.call-start = ((), (), s32[]{:S(2)}) async-start(), calls=%async_computation | async-start | bytes 1048576 | tf_op jit(solution)/shard_map/psum | solution.py:95
  8.8 5.0 %copy-start.5 = (bf16[1,1536,128]{2,1,0:T(8,128)(2,1)S(1)}, bf16[1,1536,128]{2,1,0:T(8,128)(2,1)}, u32[]{:S(2)}) copy-start(bf16[1,1536,128]{2,1,0:T(8,128)(2,1)} %param.14) | copy-start | bytes 1179652
  13.7 0.9 copy-start.4
  14.8 1.5 collective-permute-start.1
  17.2 5.4 %collective-permute-start.3 = (bf16[128,256]{1,0:T(8,128)(2,1)S(1)}, bf16[128,256]{1,0:T(8,128)(2,1)S(1)}, u32[]{:S(2)}, u32[]{:S(2)}) collective-permute-start(bf16[128,256]{1,0:T(8,128)(2,1)S(1)} %convolution_convert_fusion.3), channel_id=1, source_target_pairs={{0,2},{2,0},{1,3},{3,1},{4,6},{6,4},{5,7},{7,5},{8,10},{10,8},{9,1... | collective-permute-start | bytes 196616 | tf_op jit(solution)/shard_map/ppermute | solution.py:14
  23.6 5.3 %collective-permute-start.5 = (bf16[128,256]{1,0:T(8,128)(2,1)S(1)}, bf16[128,256]{1,0:T(8,128)(2,1)S(1)}, u32[]{:S(2)}, u32[]{:S(2)}) collective-permute-start(bf16[128,256]{1,0:T(8,128)(2,1)S(1)} %convolution_convert_fusion.2), channel_id=1, source_target_pairs={{0,4},{4,0},{1,5},{5,1},{2,6},{6,2},{3,7},{7,3},{8,12},{12,8},{9,1... | collective-permute-start | bytes 196616 | tf_op jit(solution)/shard_map/ppermute | solution.py:14
  26.5 25.9 %collective-permute-start = (bf16[128,256]{0,1:T(8,128)(2,1)S(1)}, bf16[128,256]{0,1:T(8,128)(2,1)S(1)}, u32[]{:S(2)}, u32[]{:S(2)}) collective-permute-start(bf16[128,256]{0,1:T(8,128)(2,1)S(1)} %bitcast.82), channel_id=1, source_target_pairs={{0,1},{1,0},{2,3},{3,2},{4,5},{5,4},{6,7},{7,6},{8,9},{9,8},{10,11... | collective-permute-start | bytes 196616 | tf_op jit(solution)/shard_map/ppermute | solution.py:14
  29.8 7.8 %collective-permute-start.7 = (bf16[128,256]{1,0:T(8,128)(2,1)S(1)}, bf16[128,256]{1,0:T(8,128)(2,1)S(1)}, u32[]{:S(2)}, u32[]{:S(2)}) collective-permute-start(bf16[128,256]{1,0:T(8,128)(2,1)S(1)} %convolution_convert_fusion.1), channel_id=1, source_target_pairs={{0,8},{8,0},{16,24},{24,16},{1,9},{9,1},{17,25},{25,17},{2,10},{10... | collective-permute-start | bytes 196616 | tf_op jit(solution)/shard_map/ppermute | solution.py:14
  36.9 15.6 %copy-start.3 = (bf16[1,1536,128]{2,1,0:T(8,128)(2,1)S(1)}, bf16[1,1536,128]{2,1,0:T(8,128)(2,1)}, u32[]{:S(2)}) copy-start(bf16[1,1536,128]{2,1,0:T(8,128)(2,1)} %param.15) | copy-start | bytes 1179652
  37.6 7.8 %collective-permute-start.8 = (bf16[128,256]{1,0:T(8,128)(2,1)S(1)}, bf16[128,256]{1,0:T(8,128)(2,1)S(1)}, u32[]{:S(2)}, u32[]{:S(2)}) collective-permute-start(bf16[128,256]{1,0:T(8,128)(2,1)S(1)} %add_convert_fusion.1), channel_id=1, source_target_pairs={{0,16},{16,0},{8,24},{24,8},{1,17},{17,1},{9,25},{25,9},{2,18},{18... | collective-permute-start | bytes 196616 | tf_op jit(solution)/shard_map/ppermute | solution.py:14
  40.1 11.2 %collective-permute-start.2 = (bf16[128,256]{0,1:T(8,128)(2,1)S(1)}, bf16[128,256]{0,1:T(8,128)(2,1)S(1)}, u32[]{:S(2)}, u32[]{:S(2)}) collective-permute-start(bf16[128,256]{0,1:T(8,128)(2,1)S(1)} %add_convert_fusion.4), channel_id=1, source_target_pairs={{0,2},{2,0},{1,3},{3,1},{4,6},{6,4},{5,7},{7,5},{8,10},{10,8},{9,1... | collective-permute-start | bytes 196616 | tf_op jit(solution)/shard_map/ppermute | solution.py:14
  41.7 8.5 %collective-permute-start.4 = (bf16[128,256]{1,0:T(8,128)(2,1)S(1)}, bf16[128,256]{1,0:T(8,128)(2,1)S(1)}, u32[]{:S(2)}, u32[]{:S(2)}) collective-permute-start(bf16[128,256]{1,0:T(8,128)(2,1)S(1)} %add_convert_fusion.3), channel_id=1, source_target_pairs={{0,4},{4,0},{1,5},{5,1},{2,6},{6,2},{3,7},{7,3},{8,12},{12,8},{9,1... | collective-permute-start | bytes 196616 | tf_op jit(solution)/shard_map/ppermute | solution.py:14
  44.9 4.3 %collective-permute-start.6 = (bf16[128,256]{1,0:T(8,128)(2,1)S(1)}, bf16[128,256]{1,0:T(8,128)(2,1)S(1)}, u32[]{:S(2)}, u32[]{:S(2)}) collective-permute-start(bf16[128,256]{1,0:T(8,128)(2,1)S(1)} %add_convert_fusion.2), channel_id=1, source_target_pairs={{0,8},{8,0},{16,24},{24,16},{1,9},{9,1},{17,25},{25,17},{2,10},{10... | collective-permute-start | bytes 196616 | tf_op jit(solution)/shard_map/ppermute | solution.py:14
  56.0 7.8 %copy-start.1 = (bf16[1536,256]{1,0:T(8,128)(2,1)S(1)}, bf16[1536,256]{1,0:T(8,128)(2,1)}, u32[]{:S(2)}) copy-start(bf16[1536,256]{1,0:T(8,128)(2,1)} %param.10) | copy-start | bytes 2359300
  64.1 1.1 copy-start.2
  66.3 100.6 %all-reduce.7.cloned.1.call-start = ((), (), s32[]{:S(2)}) async-start(), calls=%async_computation.1 | async-start | bytes 1048576 | tf_op jit(solution)/shard_map/psum | solution.py:95
Sparse Core Ops, SparseCore 0:
  66.5 52.9 all-reduce.4
  122.4 44.4 all-reduce.6
